TPU v7x, 256 devices: a whole 4x4x8 slice. The times are simulated.
256 devices in a mesh: section: 2 (over y_lo), dp: 4 (over y_hi, core), shard: 32 (over x, z).
Axes of the slice: x: 4, y: 4 (y_hi: 2, y_lo: 2; y = y_hi * 2 + y_lo), z: 8, core: 2. Of those that a mesh axis runs over, the one named last changes fastest.
Arguments:
- norm_input: bfloat16 [2, 4, 4096, 3584], P('section', 'dp', 'shard'), may hold values from -6 to 6
- norm_gain: float32 [2, 3584], P('section'), may hold values from 0.1 to 1.9
- branch_grad: bfloat16 [2, 4, 4096, 3584], P('section', 'dp', 'shard'), may hold values from -6 to 6
- residual_grad: bfloat16 [2, 4, 4096, 3584], P('section', 'dp', 'shard'), may hold values from -6 to 6
- down_weight: bfloat16 [2, 14336, 3584], P('section', 'shard'), may hold values from -0.09375 to 0.09375
Outputs:
- boundary_grad: bfloat16 [2, 4, 4096, 3584], P('section', 'dp', 'shard')
- gain_grad: float32 [2, 3584], P('section')
- unit_grads: bfloat16 [2, 4, 4096, 14336], P('section', 'dp', None, 'shard')
All inputs are finite; a program needn't handle non-finite values.
Results may differ from a plain program's by a relative error of at most 0.0049.
Values may be sent and summed in bfloat16 or wider, within the bound.
A program may use at most 128 MiB of HBM per device.

v0:
```python
import jax
import jax.numpy as jnp
from jax import lax
from jax.sharding import Mesh
from jax.sharding import PartitionSpec as P

DP_SHARD = ("dp_0", "dp_1", "shard_0", "shard_1")
SHARD = ("shard_0", "shard_1")
DP = ("dp_0", "dp_1")
epsilon = 1e-05


def one_axis_at_a_time(array, axes):
    for axis in axes:
        array = lax.psum(array, axis)
    return array


def from_partner(block, axis, distance):
    count = lax.axis_size(axis)
    route = []
    for low in range(count):
        high = low | 1 << distance
        if high != low and high < count:
            route += [(low, high), (high, low)]
    return lax.ppermute(block, axis, route)


def norm_backward(inputs, gain_row, branch, residual):
    values = inputs.astype(jnp.float32)
    inverse = lax.rsqrt(jnp.mean(values * values, axis=-1, keepdims=True) + epsilon)
    normed = values * inverse
    upstream = branch.astype(jnp.float32)
    scaled = upstream * gain_row
    project = jnp.mean(scaled * normed, axis=-1, keepdims=True)
    boundary = (residual.astype(jnp.float32) + inverse * (scaled - normed * project)).astype(
        jnp.bfloat16
    )
    return (boundary, jnp.sum(upstream * normed, axis=0))


def per_device(norm_input, norm_gain, branch_grad, residual_grad, down_weight):
    weight = down_weight[0]
    boundary, gain_part = norm_backward(
        norm_input[0, 0], norm_gain[0], branch_grad[0, 0], residual_grad[0, 0]
    )
    gain_total = one_axis_at_a_time(gain_part, DP_SHARD)
    arrived = from_partner(boundary, "section", 0)
    fresh = jnp.einsum(
        "nd,hd->nh",
        lax.all_gather(arrived, SHARD, axis=0, tiled=True),
        weight,
        preferred_element_type=jnp.float32,
    ).astype(jnp.bfloat16)
    gain_grad = gain_total / fresh.shape[0]
    return (boundary[None, None], gain_grad[None], fresh[None, None])


def solution(mesh):
    split = Mesh(
        mesh.devices.reshape(mesh.shape["section"], 2, 2, 4, 8),
        ("section", "dp_0", "dp_1", "shard_0", "shard_1"),
    )
    return jax.shard_map(
        per_device,
        mesh=split,
        in_specs=(
            P("section", DP, SHARD, None),
            P("section", None),
            P("section", DP, SHARD, None),
            P("section", DP, SHARD, None),
            P("section", SHARD, None),
        ),
        out_specs=(
            P("section", DP, SHARD, None),
            P("section", None),
            P("section", DP, None, SHARD),
        ),
        check_vma=False,
    )
```

profile of v0, /device:TPU:1, one launch (start us, length us, event | category | flops | bytes accessed | tf_op | source)
XLA Modules:
  0.0 275.5 jit_solution(16686822337064339081)
XLA Ops:
  7.2 0.0 copy-start
  7.2 0.0 all-gather.2.cloned.1.call-start
  7.2 1.6 fusion.17
  8.8 0.8 reduce
  9.6 0.0 copy-start.1
  9.6 0.0 copy-start.2
  9.6 2.3 fusion.16
  11.9 0.0 copy-done.1
  11.9 0.0 copy-done.2
  11.9 1.8 fusion.11
  13.8 2.2 collective-permute-start
  16.0 18.8 %collective-permute-done = bf16[128,3584]{1,0:T(8,128)(2,1)} collective-permute-done((bf16[128,3584]{1,0:T(8,128)(2,1)S(1)}, bf16[128,3584]{1,0:T(8,128)(2,1)}, u32[]{:S(2)}, u32[]{:S(2)}) %collective-permute-start) | collective-permute-done | bytes 917536 | tf_op jit(solution)/shard_map/ppermute | solution.py:26
  34.8 0.0 all-gather.2.cloned.1.call-update
  34.8 10.5 %psum.28 = f32[3584]{0:T(1024)S(1)} all-reduce(f32[3584]{0:T(1024)S(1)} %get-tuple-element.3), channel_id=1, replica_groups=mesh['section'=2,'dp_0'=2,'dp_1'=2,'shard_0'=4,'shard_1'=8] {'dp_0'}, use_global_device_ids=true, to_apply=%region_3.0 | all-reduce | flops 3584 | bytes 28672 | tf_op jit(solution)/shard_map/psum | solution.py:15
  45.4 6.7 %psum.29 = f32[3584]{0:T(1024)S(1)} all-reduce(f32[3584]{0:T(1024)S(1)} %psum.28), channel_id=1, replica_groups=mesh['section'=2,'dp_0'=2,'dp_1'=2,'shard_0'=4,'shard_1'=8] {'dp_1'}, use_global_device_ids=true, to_apply=%region_4.0 | all-reduce | flops 3584 | bytes 28672 | tf_op jit(solution)/shard_map/psum | solution.py:15
  52.1 14.8 %psum.30 = f32[3584]{0:T(1024)S(1)} all-reduce(f32[3584]{0:T(1024)S(1)} %psum.29), channel_id=1, replica_groups=mesh['section'=2,'dp_0'=2,'dp_1'=2,'shard_0'=4,'shard_1'=8] {'shard_0'}, use_global_device_ids=true, to_apply=%region_5.0 | all-reduce | flops 3584 | bytes 28672 | tf_op jit(solution)/shard_map/psum | solution.py:15
  67.0 28.4 %psum.31 = f32[3584]{0:T(1024)S(1)} all-reduce(f32[3584]{0:T(1024)S(1)} %psum.30), channel_id=1, replica_groups=mesh['section'=2,'dp_0'=2,'dp_1'=2,'shard_0'=4,'shard_1'=8] {'shard_1'}, use_global_device_ids=true, to_apply=%region_6.0 | all-reduce | flops 3584 | bytes 28672 | tf_op jit(solution)/shard_map/psum | solution.py:15
  95.4 0.6 broadcast_in_dim.4
  96.0 3.3 %fusion.12 = bf16[1,1,128,3584]{3,2,1,0:T(8,128)(2,1)} fusion(bf16[1,1,128,3584]{3,2,1,0:T(8,128)(2,1)} %param.8, bf16[1,1,128,3584]{3,2,1,0:T(8,128)(2,1)} %param.7, bf16[1,1,128,3584]{3,2,1,0:T(8,128)(2,1)} %param.5, f32[128]{0:T(128)S(1)} %broadcast_multiply_fusion.1, f32[3584]{0:T(1024)S(1)} %reduce, f32[128]{0:T(128)S(1)} %add_rsqrt_fusion), kind=kLoop, calls=%fused_computation.19 | loop fusion | flops 4587520 | bytes 3685376 | tf_op jit(solution)/shard_map/convert_element_type | solution.py:36
  99.3 149.4 %all-gather.2.cloned.1.call-done = bf16[4096,3584]{1,0:T(8,128)(2,1)} async-done(((bf16[128,3584]{1,0:T(8,128)(2,1)}), bf16[4096,3584]{1,0:T(8,128)(2,1)}) %all-gather.2.cloned.1.call-update) | async-done | bytes 29360144 | tf_op jit(solution)/shard_map/all_gather | solution.py:51
  248.7 0.0 copy-done
  248.7 20.0 %fusion = bf16[1,1,4096,448]{2,3,1,0:T(8,128)(2,1)} fusion(bf16[4096,3584]{1,0:T(8,128)(2,1)} %all-gather.2.cloned.1.call-done, bf16[1,448,3584]{2,1,0:T(8,128)(2,1)S(1)} %copy-done), kind=kOutput, calls=%fused_computation.1 | convolution fusion | flops 13155172352 | bytes 36241408 | tf_op jit(solution)/shard_map/nd,hd->nh/dot_general | solution.py:49
  (3 shorter events, 0.0 us)
Async XLA Ops:
  7.2 241.5 %copy-start = (bf16[1,448,3584]{2,1,0:T(8,128)(2,1)S(1)}, bf16[1,448,3584]{2,1,0:T(8,128)(2,1)}, u32[]{:S(2)}) copy-start(bf16[1,448,3584]{2,1,0:T(8,128)(2,1)} %param.9) | copy-start | bytes 9633796
  7.2 241.5 %all-gather.2.cloned.1.call-start = ((), (), s32[]{:S(2)}) async-start(), calls=%async_computation | async-start | bytes 30277632 | tf_op jit(solution)/shard_map/all_gather | solution.py:51
  9.6 2.3 copy-start.1
  9.6 2.3 copy-start.2
  13.8 21.0 %collective-permute-start = (bf16[128,3584]{1,0:T(8,128)(2,1)S(1)}, bf16[128,3584]{1,0:T(8,128)(2,1)}, u32[]{:S(2)}, u32[]{:S(2)}) collective-permute-start(bf16[128,3584]{1,0:T(8,128)(2,1)S(1)} %fusion.11), channel_id=1, source_target_pairs={{0,128},{128,0},{1,129},{129,1},{2,130},{130,2},{3,131},{131,3},{4... | collective-permute-start | bytes 2752520 | tf_op jit(solution)/shard_map/ppermute | solution.py:26
Sparse Core Ops, SparseCore 0:
  35.0 213.6 all-gather.1
where the time goes:
time: 276 us
  waiting for transfers between devices  168 us (61%)
  blocking collectives  60.5 us (22%)
  matrix products  20 us (7%)
  between operations  14.1 us (5%)
  other arithmetic  9.79 us (4%)
    all_gather x1, waiting for transfers between devices, per_device(): lax.all_gather(arrived, SHARD, axis=0, tiled=True)  149 us
    psum x4, blocking collectives, one_axis_at_a_time(): array = lax.psum(array, axis)  60.5 us
    dot_general x1, matrix products, per_device(): jnp.einsum('nd,hd->nh', lax.all_gather(arrived, SHARD, axis=0, tiled=True...  20 us
    ppermute x1, waiting for transfers between devices, from_partner(): return lax.ppermute(block, axis, route)  18.8 us
  transfers between devices with their start and end apart: 2, of which 2 were waited for; matrix products, arithmetic and copies ran while one was open for 1% of the time, Pallas kernels for 0%

commit v1 on v0

--- a/solution.py
+++ b/solution.py
@@ -8,6 +8,13 @@
 SHARD = ("shard_0", "shard_1")
 DP = ("dp_0", "dp_1")
 epsilon = 1e-05
+
+
+def all_by_exchange(block, name, dim):
+    size = lax.axis_size(name)
+    blocks = jnp.stack([block for _ in range(size)])
+    blocks = lax.all_to_all(blocks, name, split_axis=0, concat_axis=0)
+    return jnp.concatenate(blocks, axis=dim)
 
 
 def one_axis_at_a_time(array, axes):
@@ -47,10 +54,7 @@
     gain_total = one_axis_at_a_time(gain_part, DP_SHARD)
     arrived = from_partner(boundary, "section", 0)
     fresh = jnp.einsum(
-        "nd,hd->nh",
-        lax.all_gather(arrived, SHARD, axis=0, tiled=True),
-        weight,
-        preferred_element_type=jnp.float32,
+        "nd,hd->nh", all_by_exchange(arrived, SHARD, 0), weight, preferred_element_type=jnp.float32
     ).astype(jnp.bfloat16)
     gain_grad = gain_total / fresh.shape[0]
     return (boundary[None, None], gain_grad[None], fresh[None, None])

time: 276 us -> 802 us (2.91)
  the two profiles are of different devices: /device:TPU:1 before, /device:TPU:28 now
where the time goes in v1:
time: 802 us; the launch traced here: 801 us
  blocking collectives  726 us (91%)
  waiting for transfers between devices  21.3 us (3%)
  matrix products  20 us (2%)
  starting transfers between devices  12.5 us (2%)
  local copies, waits for them, and re-layouts  10.6 us (1%)
  other arithmetic  9.78 us (1%)
    psum x4, blocking collectives, one_axis_at_a_time(): array = lax.psum(array, axis)  726 us
    ppermute x1, waiting for transfers between devices, from_partner(): return lax.ppermute(block, axis, route)  21.3 us
    dot_general x1, matrix products, per_device(): jnp.einsum('nd,hd->nh', all_by_exchange(arrived, SHARD, 0), weight, prefe...  20 us
  transfers between devices with their start and end apart: 2, of which 1 were waited for; matrix products, arithmetic and copies ran while one was open for 0% of the time, Pallas kernels for 0%

profile of v1, /device:TPU:28, one launch (start us, length us, event | category | flops | bytes accessed | tf_op | source)
XLA Modules:
  0.0 801.3 jit_solution(7774146186817901470)
XLA Ops:
  0.6 0.0 copy-start
  0.6 1.6 fusion.17
  2.3 0.8 reduce
  3.0 0.0 copy-start.1
  3.0 0.0 copy-start.2
  3.0 2.3 fusion.16
  5.3 0.0 copy-done.1
  5.4 0.0 copy-done.2
  5.4 1.8 fusion.11
  7.2 0.8 collective-permute-start
  8.0 21.3 %collective-permute-done = bf16[128,3584]{1,0:T(8,128)(2,1)S(1)} collective-permute-done((bf16[128,3584]{1,0:T(8,128)(2,1)S(1)}, bf16[128,3584]{1,0:T(8,128)(2,1)S(1)}, u32[]{:S(2)}, u32[]{:S(2)}) %collective-permute-start) | collective-permute-done | bytes 917536 | tf_op jit(solution)/shard_map/ppermute | solution.py:33
  29.4 9.9 %stack.2 = bf16[32,128,3584]{2,1,0:T(8,128)(2,1)} broadcast(bf16[128,3584]{1,0:T(8,128)(2,1)S(1)} %collective-permute-done), dimensions={1,2} | broadcast | bytes 30277632 | tf_op jit(solution)/shard_map/stack | solution.py:15
  39.3 11.6 %all-to-all-start = ((bf16[32,128,3584]{2,1,0:T(8,128)(2,1)}), bf16[32,128,3584]{2,1,0:T(8,128)(2,1)}, u32[]{:S(2)}, u32[]{:S(2)}) async-start(bf16[32,128,3584]{2,1,0:T(8,128)(2,1)} %stack.2), calls=%async_computation | async-start | bytes 58720256 | tf_op jit(solution)/shard_map/all_to_all | solution.py:16
  50.9 9.4 %psum.28 = f32[3584]{0:T(1024)S(1)} all-reduce(f32[3584]{0:T(1024)S(1)} %get-tuple-element.3), channel_id=1, replica_groups=mesh['section'=2,'dp_0'=2,'dp_1'=2,'shard_0'=4,'shard_1'=8] {'dp_0'}, use_global_device_ids=true, to_apply=%region_3.0 | all-reduce | flops 3584 | bytes 28672 | tf_op jit(solution)/shard_map/psum | solution.py:22
  60.3 3.3 psum.29
  63.7 53.8 %psum.30 = f32[3584]{0:T(1024)S(1)} all-reduce(f32[3584]{0:T(1024)S(1)} %psum.29), channel_id=1, replica_groups=mesh['section'=2,'dp_0'=2,'dp_1'=2,'shard_0'=4,'shard_1'=8] {'shard_0'}, use_global_device_ids=true, to_apply=%region_5.0 | all-reduce | flops 3584 | bytes 28672 | tf_op jit(solution)/shard_map/psum | solution.py:22
  117.5 659.8 %psum.31 = f32[3584]{0:T(1024)S(1)} all-reduce(f32[3584]{0:T(1024)S(1)} %psum.30), channel_id=1, replica_groups=mesh['section'=2,'dp_0'=2,'dp_1'=2,'shard_0'=4,'shard_1'=8] {'shard_1'}, use_global_device_ids=true, to_apply=%region_6.0 | all-reduce | flops 3584 | bytes 28672 | tf_op jit(solution)/shard_map/psum | solution.py:22
  777.3 0.6 broadcast_in_dim.4
  777.9 3.3 fusion.12
  781.2 0.0 all-to-all-done
  781.2 0.0 copy-done
  781.2 20.0 %fusion = bf16[1,1,4096,448]{2,3,1,0:T(8,128)(2,1)} fusion(bf16[4096,3584]{1,0:T(8,128)(2,1)} %bitcast.3, bf16[1,448,3584]{2,1,0:T(8,128)(2,1)S(1)} %copy-done), kind=kOutput, calls=%fused_computation.1 | convolution fusion | flops 13155172352 | bytes 36241408 | tf_op jit(solution)/shard_map/nd,hd->nh/dot_general | solution.py:56
  (3 shorter events, 0.0 us)
Async XLA Ops:
  0.6 780.6 %copy-start = (bf16[1,448,3584]{2,1,0:T(8,128)(2,1)S(1)}, bf16[1,448,3584]{2,1,0:T(8,128)(2,1)}, u32[]{:S(2)}) copy-start(bf16[1,448,3584]{2,1,0:T(8,128)(2,1)} %param.9) | copy-start | bytes 9633796
  3.0 2.3 copy-start.1
  3.0 2.3 copy-start.2
  7.2 22.2 %collective-permute-start = (bf16[128,3584]{1,0:T(8,128)(2,1)S(1)}, bf16[128,3584]{1,0:T(8,128)(2,1)S(1)}, u32[]{:S(2)}, u32[]{:S(2)}) collective-permute-start(bf16[128,3584]{1,0:T(8,128)(2,1)S(1)} %fusion.11), channel_id=1, source_target_pairs={{0,128},{128,0},{1,129},{129,1},{2,130},{130,2},{3,131},{131,3},{4... | collective-permute-start | bytes 2752520 | tf_op jit(solution)/shard_map/ppermute | solution.py:33
  39.3 741.9 %all-to-all-start = ((bf16[32,128,3584]{2,1,0:T(8,128)(2,1)}), bf16[32,128,3584]{2,1,0:T(8,128)(2,1)}, u32[]{:S(2)}, u32[]{:S(2)}) async-start(bf16[32,128,3584]{2,1,0:T(8,128)(2,1)} %stack.2), calls=%async_computation | async-start | bytes 58720256 | tf_op jit(solution)/shard_map/all_to_all | solution.py:16
